TPU v7x, 512 devices: a whole 4x8x8 slice. The times are simulated.
512 devices in a mesh: fsdp: 16 (over y, core), ctx: 32 (over z, x).
Axes of the slice: x: 4, y: 8, z: 8, core: 2. Of those that a mesh axis runs over, the one named last changes fastest.
Arguments:
- featurized: bfloat16 [4096, 3, 4096], P('ctx', None, 'fsdp'), may hold values from -6 to 6
- short_taps: float32 [3, 3, 4096], P(None, None, 'fsdp'), may hold values from -3 to 3
- residues: float32 [4096, 16], P('fsdp'), may hold values from -1.5 to 1.5
- decay_rates: float32 [4096, 16], P('fsdp'), may hold values from 0.00012207031 to 0.05
- w_out: bfloat16 [4096, 8192], P('fsdp', 'ctx'), may hold values from -0.09375 to 0.09375
- grad_out: bfloat16 [4096, 8192], P('ctx'), may hold values from -6 to 6
Outputs:
- block_output: bfloat16 [4096, 8192], P('ctx', 'fsdp')
- grad_features: bfloat16 [4096, 3, 4096], P('ctx', None, 'fsdp')
All inputs are finite; a program needn't handle non-finite values.
Results may differ from a plain program's by a relative error of at most 0.02.
Values may be sent and summed in bfloat16 or wider, within the bound.
A program may use at most 64 MiB of HBM per device.

v0:
```python
import math
import jax
import jax.numpy as jnp
from jax import lax
from jax.sharding import PartitionSpec as P

HIGHEST = lax.Precision.HIGHEST


def swapped(block, axis, distance):
    count = lax.axis_size(axis)
    route = []
    for low in range(count):
        high = low | 1 << distance
        if high != low and high < count:
            route += [(low, high), (high, low)]
    return lax.ppermute(block, axis, route)


def shifted(block, axis, distance):
    devices = range(lax.axis_size(axis))
    route = [(i - distance, i) for i in devices if i - distance in devices]
    return lax.ppermute(block, axis, route)


def angles(product_index, modulus):
    phases = (product_index % modulus).astype(jnp.float32) * (2.0 * math.pi / modulus)
    return (jnp.cos(phases), jnp.sin(phases))


def complex_contract(pattern, table_re, table_im, real_part, imag_part):
    first_term = jnp.einsum(pattern, table_re, real_part, precision=HIGHEST)
    second_term = jnp.einsum(pattern, table_im, imag_part, precision=HIGHEST)
    third_term = jnp.einsum(pattern, table_re, imag_part, precision=HIGHEST)
    fourth_term = jnp.einsum(pattern, table_im, real_part, precision=HIGHEST)
    return (first_term - second_term, third_term + fourth_term)


def token_tables(tokens_here):
    positions_all = jnp.arange(tokens_here)
    return angles(positions_all[:, None] * positions_all[None, :], tokens_here)


def reversed_bits(my_rank, bit_count):
    result = jnp.zeros((), jnp.int32)
    for section_bit in range(bit_count):
        result = result + (my_rank >> section_bit & 1) * (1 << bit_count - 1 - section_bit)
    return result


def partner_step(values_now, section_bit, my_rank, inverse):
    partner_data = swapped(values_now.astype(jnp.bfloat16), "ctx", section_bit).astype(
        values_now.dtype
    )
    half_span = 1 << section_bit
    upper_side = my_rank >> section_bit & 1 == 1
    cos_turn, sin_turn = angles(my_rank % half_span, 2 * half_span)
    if inverse:
        spun_re = partner_data[0] * cos_turn - partner_data[1] * sin_turn
        spun_im = partner_data[1] * cos_turn + partner_data[0] * sin_turn
        lower_new = jnp.stack([values_now[0] + spun_re, values_now[1] + spun_im]) * 0.5
        mine_re = values_now[0] * cos_turn - values_now[1] * sin_turn
        mine_im = values_now[1] * cos_turn + values_now[0] * sin_turn
        upper_new = jnp.stack([partner_data[0] - mine_re, partner_data[1] - mine_im]) * 0.5
    else:
        lower_new = values_now + partner_data
        differ = partner_data - values_now
        upper_new = jnp.stack(
            [
                differ[0] * cos_turn + differ[1] * sin_turn,
                differ[1] * cos_turn - differ[0] * sin_turn,
            ]
        )
    return jnp.where(upper_side, upper_new, lower_new)


def forward_partners(signal):
    tokens_here = signal.shape[0]
    devices = lax.axis_size("ctx")
    bit_count = devices.bit_length() - 1
    my_rank = lax.axis_index("ctx")
    full_length = 2 * devices * tokens_here
    half_turn = my_rank.astype(jnp.float32) * (math.pi / devices)
    values_now = jnp.stack(
        [
            jnp.stack([signal, signal * jnp.cos(half_turn)]),
            jnp.stack([jnp.zeros_like(signal), -signal * jnp.sin(half_turn)]),
        ]
    )
    for section_bit in reversed(range(bit_count)):
        values_now = partner_step(values_now, section_bit, my_rank, False)
    spectral_rows = 2 * reversed_bits(my_rank, bit_count) + jnp.arange(2)
    cos_twist, sin_twist = angles(
        spectral_rows[:, None] * jnp.arange(tokens_here)[None, :], full_length
    )
    cos_twist = cos_twist[:, :, None, None]
    sin_twist = sin_twist[:, :, None, None]
    twist_re = values_now[0] * cos_twist + values_now[1] * sin_twist
    twist_im = values_now[1] * cos_twist - values_now[0] * sin_twist
    cos_tokens, sin_tokens = token_tables(tokens_here)
    return complex_contract("ks,esgc->ekgc", cos_tokens, -sin_tokens, twist_re, twist_im)


def inverse_partners(spec_re, spec_im):
    tokens_here = spec_re.shape[1]
    devices = lax.axis_size("ctx")
    bit_count = devices.bit_length() - 1
    my_rank = lax.axis_index("ctx")
    full_length = 2 * devices * tokens_here
    cos_tokens, sin_tokens = token_tables(tokens_here)
    plain_re, plain_im = complex_contract("sk,ekgc->esgc", cos_tokens, sin_tokens, spec_re, spec_im)
    spectral_rows = 2 * reversed_bits(my_rank, bit_count) + jnp.arange(2)
    cos_twist, sin_twist = angles(
        spectral_rows[:, None] * jnp.arange(tokens_here)[None, :], full_length
    )
    cos_twist = cos_twist[:, :, None, None]
    sin_twist = sin_twist[:, :, None, None]
    twist_re = plain_re * cos_twist - plain_im * sin_twist
    twist_im = plain_re * sin_twist + plain_im * cos_twist
    values_now = jnp.stack([twist_re, twist_im])
    for section_bit in range(bit_count):
        values_now = partner_step(values_now, section_bit, my_rank, True)
    half_turn = my_rank.astype(jnp.float32) * (math.pi / devices)
    real_part = (
        values_now[0, 0]
        + values_now[0, 1] * jnp.cos(half_turn)
        - values_now[1, 1] * jnp.sin(half_turn)
    )
    return real_part / (2.0 * tokens_here)


def to_spectrum(signal):
    return forward_partners(signal)


def from_spectrum(spec_re, spec_im):
    return inverse_partners(spec_re, spec_im)


def modal_spectrum(residues, decay_rates, spectral_rows, tokens_here, devices):
    full_length = 2 * devices * tokens_here
    sequence = devices * tokens_here
    frequency = spectral_rows[:, None] + 2 * devices * jnp.arange(tokens_here)[None, :]
    angle_now = frequency.astype(jnp.float32) * (math.pi / full_length)
    half_sine = jnp.sin(angle_now)[:, :, None]
    full_sine = jnp.sin(2.0 * angle_now)[:, :, None]
    parity_sign = (1 - 2 * (spectral_rows % 2)).astype(jnp.float32)[:, None, None]

    def add_mode(mode_index, totals):
        rates_now = lax.dynamic_slice_in_dim(decay_rates, mode_index, 1, 1)[:, 0]
        weight = lax.dynamic_slice_in_dim(residues, mode_index, 1, 1)[:, 0] * jnp.sqrt(rates_now)
        decay_now = jnp.exp(-rates_now)
        numerator = 1.0 - parity_sign * jnp.exp(-rates_now * sequence)
        denom_re = -jnp.expm1(-rates_now) + 2.0 * decay_now * half_sine * half_sine
        denom_im = decay_now * full_sine
        scaled = weight * numerator / (denom_re * denom_re + denom_im * denom_im)
        return (totals[0] + scaled * denom_re, totals[1] - scaled * denom_im)

    empty = jnp.zeros((spectral_rows.shape[0], tokens_here, residues.shape[0]), jnp.float32)
    spec_re, spec_im = lax.fori_loop(0, residues.shape[1], add_mode, (empty, empty))
    return (spec_re[:, :, None, :], spec_im[:, :, None, :])


def own_filter(residues, decay_rates, tokens_here):
    devices = lax.axis_size("ctx")
    my_rank = lax.axis_index("ctx")
    pair_rank = reversed_bits(my_rank, devices.bit_length() - 1)
    return modal_spectrum(
        residues, decay_rates, 2 * pair_rank + jnp.arange(2), tokens_here, devices
    )


def per_device(featurized, short_taps, residues, decay_rates, w_out, grad_out):
    tokens_here = featurized.shape[0]
    before = shifted(featurized[tokens_here - 2 :], "ctx", 1)
    raw_values = featurized.astype(jnp.float32)
    extended = jnp.concatenate([before.astype(jnp.float32), raw_values], axis=0)
    mixed_in = (
        short_taps[0] * extended[2:]
        + short_taps[1] * extended[1 : tokens_here + 1]
        + short_taps[2] * extended[:tokens_here]
    )
    query_part = mixed_in[:, 0]
    key_part = mixed_in[:, 1]
    value_part = mixed_in[:, 2]
    carried = key_part * value_part
    signal_re, signal_im = to_spectrum(carried[:, None, :])
    filter_re, filter_im = own_filter(residues, decay_rates, tokens_here)
    conv_re = signal_re * filter_re - signal_im * filter_im
    conv_im = signal_re * filter_im + signal_im * filter_re
    convolved = from_spectrum(conv_re, conv_im)[:, 0]
    gated_out = (query_part * convolved).astype(jnp.bfloat16)
    w_full = lax.all_gather(w_out, "ctx", axis=1, tiled=True)
    partial_sum = jnp.dot(gated_out, w_full, preferred_element_type=jnp.float32)
    block_output = lax.psum_scatter(
        partial_sum.astype(jnp.bfloat16), "fsdp", scatter_dimension=1, tiled=True
    )
    grad_gated = lax.dot_general(
        grad_out, w_full, (((1,), (1,)), ((), ())), preferred_element_type=jnp.float32
    )
    grad_query = grad_gated * convolved
    grad_conv = grad_gated * query_part
    delta_re, delta_im = to_spectrum(grad_conv[:, None, :])
    back_re = filter_re * delta_re + filter_im * delta_im
    back_im = filter_re * delta_im - filter_im * delta_re
    grad_carried = from_spectrum(back_re, back_im)[:, 0]
    grad_mixed = jnp.stack([grad_query, grad_carried * value_part, grad_carried * key_part], axis=1)
    following = shifted(grad_mixed[:2], "ctx", -1)
    padded = jnp.concatenate([grad_mixed, following], axis=0)
    grad_features = (
        short_taps[0] * padded[:tokens_here]
        + short_taps[1] * padded[1 : tokens_here + 1]
        + short_taps[2] * padded[2:]
    ).astype(jnp.bfloat16)
    return (block_output, grad_features)


def solution(mesh):
    placed = (
        P("ctx", None, "fsdp"),
        P(None, None, "fsdp"),
        P("fsdp", None),
        P("fsdp", None),
        P("fsdp", "ctx"),
        P("ctx", None),
    )
    return jax.shard_map(
        per_device,
        mesh=mesh,
        in_specs=placed,
        out_specs=(P("ctx", "fsdp"), P("ctx", None, "fsdp")),
        check_vma=False,
    )
```

profile of v0, /device:TPU:25, one launch (start us, length us, event | category | flops | bytes accessed | tf_op | source)
XLA Modules:
  0.0 354.1 jit_solution(11547537968246586453)
XLA Ops:
  15.2 12.7 %collective-permute-start.1 = (bf16[2,2,128,1,256]{4,2,1,3,0:T(8,128)(2,1)}, bf16[2,2,128,1,256]{4,2,1,3,0:T(8,128)(2,1)}, u32[]{:S(2)}, u32[]{:S(2)}) collective-permute-start(bf16[2,2,128,1,256]{4,2,1,3,0:T(8,128)(2,1)} %fusion.53), channel_id=1, source_target_pairs={{0,16},{16,0},{1,17},{17,1},{2,18},{18,2},{3,19},{19,3},{4,20},{20... | collective-permute-start | bytes 786440 | tf_op jit(solution)/shard_map/ppermute | solution.py:17
  27.9 78.2 %all-gather.2.cloned.1.call-done = bf16[256,8192]{1,0:T(8,128)(2,1)} async-done(((bf16[256,256]{1,0:T(8,128)(2,1)}), bf16[256,8192]{1,0:T(8,128)(2,1)}) %all-gather.2.cloned.1.call-update) | async-done | bytes 4194320 | tf_op jit(solution)/shard_map/all_gather | solution.py:193
  110.5 4.2 %collective-permute-start.11 = (bf16[2,2,128,1,256]{4,2,1,3,0:T(8,128)(2,1)S(1)}, bf16[2,2,128,1,256]{4,2,1,3,0:T(8,128)(2,1)S(1)}, u32[]{:S(2)}, u32[]{:S(2)}) collective-permute-start(bf16[2,2,128,1,256]{4,2,1,3,0:T(8,128)(2,1)S(1)} %fusion.52), channel_id=1, source_target_pairs={{0,16},{16,0},{1,17},{17,1},{2,18},{18,2},{3,19},{19,3},{4,20},{20... | collective-permute-start | bytes 786440 | tf_op jit(solution)/shard_map/ppermute | solution.py:17
  114.8 29.6 %while.18 = (s32[]{:T(128)}, f32[2,128,256]{2,1,0:T(8,128)S(1)}, f32[2,128,256]{2,1,0:T(8,128)S(1)}, f32[256,16]{0,1:T(8,128)}, f32[256,16]{0,1:T(8,128)}, /*ind...) while((s32[]{:T(128)}, f32[2,128,256]{2,1,0:T(8,128)S(1)}, ...), condition=%wide.region_1.2_spmd.clone.clone.clone, body=%wide.region_0.1_spmd.clone.clone.clone.sunk | while | flops 921377 | bytes 1070735 | solution.py:160
  148.3 3.9 %collective-permute-start.2 = (bf16[2,2,128,1,256]{4,2,1,3,0:T(8,128)(2,1)}, bf16[2,2,128,1,256]{4,2,1,3,0:T(8,128)(2,1)S(1)}, u32[]{:S(2)}, u32[]{:S(2)}) collective-permute-start(bf16[2,2,128,1,256]{4,2,1,3,0:T(8,128)(2,1)} %get-tuple-element.293), channel_id=1, source_target_pairs={{0,8},{8,0},{1,9},{9,1},{2,10},{10,2},{3,11},{11,3},{4,12},{12,4},... | collective-permute-start | bytes 786440 | tf_op jit(solution)/shard_map/ppermute | solution.py:17
  156.6 8.9 %collective-permute-done.2 = bf16[2,2,128,1,256]{4,2,1,3,0:T(8,128)(2,1)S(1)} collective-permute-done((bf16[2,2,128,1,256]{4,2,1,3,0:T(8,128)(2,1)}, bf16[2,2,128,1,256]{4,2,1,3,0:T(8,128)(2,1)S(1)}, u32[]{:S(2)}, u32[]{:S(2)}) %collective-permute-start.2) | collective-permute-done | bytes 262176 | tf_op jit(solution)/shard_map/ppermute | solution.py:17
  167.7 6.3 %collective-permute-done.12 = bf16[2,2,128,1,256]{4,2,1,3,0:T(8,128)(2,1)S(1)} collective-permute-done((bf16[2,2,128,1,256]{4,2,1,3,0:T(8,128)(2,1)S(1)}, bf16[2,2,128,1,256]{4,2,1,3,0:T(8,128)(2,1)S(1)}, u32[]{:S(2)}, u32[]{:S(2)}) %collective-permute-start.12) | collective-permute-done | bytes 262176 | tf_op jit(solution)/shard_map/ppermute | solution.py:17
  179.6 4.4 %collective-permute-start.4 = (bf16[2,2,128,1,256]{4,2,1,3,0:T(8,128)(2,1)S(1)}, bf16[2,2,128,1,256]{4,2,1,3,0:T(8,128)(2,1)S(1)}, u32[]{:S(2)}, u32[]{:S(2)}) collective-permute-start(bf16[2,2,128,1,256]{4,2,1,3,0:T(8,128)(2,1)S(1)} %get-tuple-element.289), channel_id=1, source_target_pairs={{0,2},{2,0},{1,3},{3,1},{4,6},{6,4},{5,7},{7,5},{8,10},{10,8},{9,1... | collective-permute-start | bytes 786440 | tf_op jit(solution)/shard_map/ppermute | solution.py:17
  185.2 4.7 %collective-permute-start.14 = (bf16[2,2,128,1,256]{4,2,1,3,0:T(8,128)(2,1)S(1)}, bf16[2,2,128,1,256]{4,2,1,3,0:T(8,128)(2,1)S(1)}, u32[]{:S(2)}, u32[]{:S(2)}) collective-permute-start(bf16[2,2,128,1,256]{4,2,1,3,0:T(8,128)(2,1)S(1)} %get-tuple-element.269), channel_id=1, source_target_pairs={{0,2},{2,0},{1,3},{3,1},{4,6},{6,4},{5,7},{7,5},{8,10},{10,8},{9,1... | collective-permute-start | bytes 786440 | tf_op jit(solution)/shard_map/ppermute | solution.py:17
  192.1 4.1 %collective-permute-done.14 = bf16[2,2,128,1,256]{4,2,1,3,0:T(8,128)(2,1)S(1)} collective-permute-done((bf16[2,2,128,1,256]{4,2,1,3,0:T(8,128)(2,1)S(1)}, bf16[2,2,128,1,256]{4,2,1,3,0:T(8,128)(2,1)S(1)}, u32[]{:S(2)}, u32[]{:S(2)}) %collective-permute-start.14) | collective-permute-done | bytes 262176 | tf_op jit(solution)/shard_map/ppermute | solution.py:17
  203.1 3.9 %collective-permute-done.15 = bf16[2,2,128,1,256]{4,2,1,3,0:T(8,128)(2,1)S(1)} collective-permute-done((bf16[2,2,128,1,256]{4,2,1,3,0:T(8,128)(2,1)S(1)}, bf16[2,2,128,1,256]{4,2,1,3,0:T(8,128)(2,1)S(1)}, u32[]{:S(2)}, u32[]{:S(2)}) %collective-permute-start.15) | collective-permute-done | bytes 262176 | tf_op jit(solution)/shard_map/ppermute | solution.py:17
  226.6 8.3 %collective-permute-done.7 = bf16[2,2,128,1,256]{4,2,1,3,0:T(8,128)(2,1)S(1)} collective-permute-done((bf16[2,2,128,1,256]{4,2,1,3,0:T(8,128)(2,1)S(1)}, bf16[2,2,128,1,256]{4,2,1,3,0:T(8,128)(2,1)S(1)}, u32[]{:S(2)}, u32[]{:S(2)}) %collective-permute-start.7) | collective-permute-done | bytes 262176 | tf_op jit(solution)/shard_map/ppermute | solution.py:17
  237.4 5.0 %collective-permute-done.8 = bf16[2,2,128,1,256]{4,2,1,3,0:T(8,128)(2,1)S(1)} collective-permute-done((bf16[2,2,128,1,256]{4,2,1,3,0:T(8,128)(2,1)S(1)}, bf16[2,2,128,1,256]{4,2,1,3,0:T(8,128)(2,1)S(1)}, u32[]{:S(2)}, u32[]{:S(2)}) %collective-permute-start.8) | collective-permute-done | bytes 262176 | tf_op jit(solution)/shard_map/ppermute | solution.py:17
  244.9 8.4 %collective-permute-done.9 = bf16[2,2,128,1,256]{4,2,1,3,0:T(8,128)(2,1)S(1)} collective-permute-done((bf16[2,2,128,1,256]{4,2,1,3,0:T(8,128)(2,1)S(1)}, bf16[2,2,128,1,256]{4,2,1,3,0:T(8,128)(2,1)S(1)}, u32[]{:S(2)}, u32[]{:S(2)}) %collective-permute-start.9) | collective-permute-done | bytes 262176 | tf_op jit(solution)/shard_map/ppermute | solution.py:17
  253.6 4.8 %collective-permute-start.10 = (bf16[2,2,128,1,256]{4,2,1,3,0:T(8,128)(2,1)S(1)}, bf16[2,2,128,1,256]{4,2,1,3,0:T(8,128)(2,1)S(1)}, u32[]{:S(2)}, u32[]{:S(2)}) collective-permute-start(bf16[2,2,128,1,256]{4,2,1,3,0:T(8,128)(2,1)S(1)} %get-tuple-element.275), channel_id=1, source_target_pairs={{0,16},{16,0},{1,17},{17,1},{2,18},{18,2},{3,19},{19,3},{4,20},{20... | collective-permute-start | bytes 786440 | tf_op jit(solution)/shard_map/ppermute | solution.py:17
  261.1 4.3 %collective-permute-done.10 = bf16[2,2,128,1,256]{4,2,1,3,0:T(8,128)(2,1)S(1)} collective-permute-done((bf16[2,2,128,1,256]{4,2,1,3,0:T(8,128)(2,1)S(1)}, bf16[2,2,128,1,256]{4,2,1,3,0:T(8,128)(2,1)S(1)}, u32[]{:S(2)}, u32[]{:S(2)}) %collective-permute-start.10) | collective-permute-done | bytes 262176 | tf_op jit(solution)/shard_map/ppermute | solution.py:17
  268.1 6.3 %collective-permute-start.17 = (bf16[2,2,128,1,256]{4,2,1,3,0:T(8,128)(2,1)S(1)}, bf16[2,2,128,1,256]{4,2,1,3,0:T(8,128)(2,1)S(1)}, u32[]{:S(2)}, u32[]{:S(2)}) collective-permute-start(bf16[2,2,128,1,256]{4,2,1,3,0:T(8,128)(2,1)S(1)} %get-tuple-element.261), channel_id=1, source_target_pairs={{0,2},{2,0},{1,3},{3,1},{4,6},{6,4},{5,7},{7,5},{8,10},{10,8},{9,1... | collective-permute-start | bytes 786440 | tf_op jit(solution)/shard_map/ppermute | solution.py:17
  274.4 4.0 %collective-permute-done.17 = bf16[2,2,128,1,256]{4,2,1,3,0:T(8,128)(2,1)S(1)} collective-permute-done((bf16[2,2,128,1,256]{4,2,1,3,0:T(8,128)(2,1)S(1)}, bf16[2,2,128,1,256]{4,2,1,3,0:T(8,128)(2,1)S(1)}, u32[]{:S(2)}, u32[]{:S(2)}) %collective-permute-start.17) | collective-permute-done | bytes 262176 | tf_op jit(solution)/shard_map/ppermute | solution.py:17
  281.9 3.9 %collective-permute-done.18 = bf16[2,2,128,1,256]{4,2,1,3,0:T(8,128)(2,1)S(1)} collective-permute-done((bf16[2,2,128,1,256]{4,2,1,3,0:T(8,128)(2,1)S(1)}, bf16[2,2,128,1,256]{4,2,1,3,0:T(8,128)(2,1)S(1)}, u32[]{:S(2)}, u32[]{:S(2)}) %collective-permute-start.18) | collective-permute-done | bytes 262176 | tf_op jit(solution)/shard_map/ppermute | solution.py:17
  286.0 4.9 %collective-permute-start.19 = (bf16[2,2,128,1,256]{4,2,1,3,0:T(8,128)(2,1)S(1)}, bf16[2,2,128,1,256]{4,2,1,3,0:T(8,128)(2,1)S(1)}, u32[]{:S(2)}, u32[]{:S(2)}) collective-permute-start(bf16[2,2,128,1,256]{4,2,1,3,0:T(8,128)(2,1)S(1)} %get-tuple-element.257), channel_id=1, source_target_pairs={{0,8},{8,0},{1,9},{9,1},{2,10},{10,2},{3,11},{11,3},{4,12},{12,4},... | collective-permute-start | bytes 786440 | tf_op jit(solution)/shard_map/ppermute | solution.py:17
  290.9 6.6 %collective-permute-done.19 = bf16[2,2,128,1,256]{4,2,1,3,0:T(8,128)(2,1)S(1)} collective-permute-done((bf16[2,2,128,1,256]{4,2,1,3,0:T(8,128)(2,1)S(1)}, bf16[2,2,128,1,256]{4,2,1,3,0:T(8,128)(2,1)S(1)}, u32[]{:S(2)}, u32[]{:S(2)}) %collective-permute-start.19) | collective-permute-done | bytes 262176 | tf_op jit(solution)/shard_map/ppermute | solution.py:17
  297.8 5.7 %collective-permute-start.20 = (bf16[2,2,128,1,256]{4,2,1,3,0:T(8,128)(2,1)S(1)}, bf16[2,2,128,1,256]{4,2,1,3,0:T(8,128)(2,1)S(1)}, u32[]{:S(2)}, u32[]{:S(2)}) collective-permute-start(bf16[2,2,128,1,256]{4,2,1,3,0:T(8,128)(2,1)S(1)} %get-tuple-element.255), channel_id=1, source_target_pairs={{0,16},{16,0},{1,17},{17,1},{2,18},{18,2},{3,19},{19,3},{4,20},{20... | collective-permute-start | bytes 786440 | tf_op jit(solution)/shard_map/ppermute | solution.py:17
  303.5 7.9 %collective-permute-done.20 = bf16[2,2,128,1,256]{4,2,1,3,0:T(8,128)(2,1)S(1)} collective-permute-done((bf16[2,2,128,1,256]{4,2,1,3,0:T(8,128)(2,1)S(1)}, bf16[2,2,128,1,256]{4,2,1,3,0:T(8,128)(2,1)S(1)}, u32[]{:S(2)}, u32[]{:S(2)}) %collective-permute-start.20) | collective-permute-done | bytes 262176 | tf_op jit(solution)/shard_map/ppermute | solution.py:17
  317.4 29.9 %reduce-scatter.2.cloned.1.call-done = bf16[128,512]{1,0:T(8,128)(2,1)} async-done(((bf16[128,8192]{1,0:T(8,128)(2,1)}), bf16[128,512]{1,0:T(8,128)(2,1)}) %reduce-scatter.2.cloned.1.call-update) | async-done | bytes 131088 | tf_op jit(solution)/shard_map/reduce_scatter | solution.py:195
  (239 shorter events, 106.3 us)
Async XLA Ops:
  7.2 98.9 %all-gather.2.cloned.1.call-start = ((), (), s32[]{:S(2)}) async-start(), calls=%async_computation.1 | async-start | bytes 4325376 | tf_op jit(solution)/shard_map/all_gather | solution.py:193
  7.9 339.4 %reduce-scatter.2.cloned.1.call-start = ((), (), s32[]{:S(2)}) async-start(), calls=%async_computation.2 | async-start | bytes 2228224 | tf_op jit(solution)/shard_map/reduce_scatter | solution.py:195
  8.7 5.6 %collective-permute-start = (bf16[2,3,256]{2,0,1:T(2,128)(2,1)S(1)}, bf16[2,3,256]{2,0,1:T(2,128)(2,1)S(1)}, u32[]{:S(2)}, u32[]{:S(2)}) collective-permute-start(bf16[2,3,256]{2,0,1:T(2,128)(2,1)S(1)} %slice.158), channel_id=1, source_target_pairs={{0,1},{1,2},{2,3},{3,4},{4,5},{5,6},{6,7},{7,8},{8,9},{9,10},{10,1... | collective-permute-start | bytes 9224 | tf_op jit(solution)/shard_map/ppermute | solution.py:23
  15.2 129.3 %collective-permute-start.1 = (bf16[2,2,128,1,256]{4,2,1,3,0:T(8,128)(2,1)}, bf16[2,2,128,1,256]{4,2,1,3,0:T(8,128)(2,1)}, u32[]{:S(2)}, u32[]{:S(2)}) collective-permute-start(bf16[2,2,128,1,256]{4,2,1,3,0:T(8,128)(2,1)} %fusion.53), channel_id=1, source_target_pairs={{0,16},{16,0},{1,17},{17,1},{2,18},{18,2},{3,19},{19,3},{4,20},{20... | collective-permute-start | bytes 786440 | tf_op jit(solution)/shard_map/ppermute | solution.py:17
  110.5 35.0 %collective-permute-start.11 = (bf16[2,2,128,1,256]{4,2,1,3,0:T(8,128)(2,1)S(1)}, bf16[2,2,128,1,256]{4,2,1,3,0:T(8,128)(2,1)S(1)}, u32[]{:S(2)}, u32[]{:S(2)}) collective-permute-start(bf16[2,2,128,1,256]{4,2,1,3,0:T(8,128)(2,1)S(1)} %fusion.52), channel_id=1, source_target_pairs={{0,16},{16,0},{1,17},{17,1},{2,18},{18,2},{3,19},{19,3},{4,20},{20... | collective-permute-start | bytes 786440 | tf_op jit(solution)/shard_map/ppermute | solution.py:17
  148.3 17.2 %collective-permute-start.2 = (bf16[2,2,128,1,256]{4,2,1,3,0:T(8,128)(2,1)}, bf16[2,2,128,1,256]{4,2,1,3,0:T(8,128)(2,1)S(1)}, u32[]{:S(2)}, u32[]{:S(2)}) collective-permute-start(bf16[2,2,128,1,256]{4,2,1,3,0:T(8,128)(2,1)} %get-tuple-element.293), channel_id=1, source_target_pairs={{0,8},{8,0},{1,9},{9,1},{2,10},{10,2},{3,11},{11,3},{4,12},{12,4},... | collective-permute-start | bytes 786440 | tf_op jit(solution)/shard_map/ppermute | solution.py:17
  154.3 19.7 %collective-permute-start.12 = (bf16[2,2,128,1,256]{4,2,1,3,0:T(8,128)(2,1)S(1)}, bf16[2,2,128,1,256]{4,2,1,3,0:T(8,128)(2,1)S(1)}, u32[]{:S(2)}, u32[]{:S(2)}) collective-permute-start(bf16[2,2,128,1,256]{4,2,1,3,0:T(8,128)(2,1)S(1)} %get-tuple-element.273), channel_id=1, source_target_pairs={{0,8},{8,0},{1,9},{9,1},{2,10},{10,2},{3,11},{11,3},{4,12},{12,4},... | collective-permute-start | bytes 786440 | tf_op jit(solution)/shard_map/ppermute | solution.py:17
  165.7 13.6 %collective-permute-start.3 = (bf16[2,2,128,1,256]{4,2,1,3,0:T(8,128)(2,1)S(1)}, bf16[2,2,128,1,256]{4,2,1,3,0:T(8,128)(2,1)S(1)}, u32[]{:S(2)}, u32[]{:S(2)}) collective-permute-start(bf16[2,2,128,1,256]{4,2,1,3,0:T(8,128)(2,1)S(1)} %get-tuple-element.291), channel_id=1, source_target_pairs={{0,4},{4,0},{1,5},{5,1},{2,6},{6,2},{3,7},{7,3},{8,12},{12,8},{9,1... | collective-permute-start | bytes 786440 | tf_op jit(solution)/shard_map/ppermute | solution.py:17
  174.2 10.8 %collective-permute-start.13 = (bf16[2,2,128,1,256]{4,2,1,3,0:T(8,128)(2,1)S(1)}, bf16[2,2,128,1,256]{4,2,1,3,0:T(8,128)(2,1)S(1)}, u32[]{:S(2)}, u32[]{:S(2)}) collective-permute-start(bf16[2,2,128,1,256]{4,2,1,3,0:T(8,128)(2,1)S(1)} %get-tuple-element.271), channel_id=1, source_target_pairs={{0,4},{4,0},{1,5},{5,1},{2,6},{6,2},{3,7},{7,3},{8,12},{12,8},{9,1... | collective-permute-start | bytes 786440 | tf_op jit(solution)/shard_map/ppermute | solution.py:17
  179.6 10.3 %collective-permute-start.4 = (bf16[2,2,128,1,256]{4,2,1,3,0:T(8,128)(2,1)S(1)}, bf16[2,2,128,1,256]{4,2,1,3,0:T(8,128)(2,1)S(1)}, u32[]{:S(2)}, u32[]{:S(2)}) collective-permute-start(bf16[2,2,128,1,256]{4,2,1,3,0:T(8,128)(2,1)S(1)} %get-tuple-element.289), channel_id=1, source_target_pairs={{0,2},{2,0},{1,3},{3,1},{4,6},{6,4},{5,7},{7,5},{8,10},{10,8},{9,1... | collective-permute-start | bytes 786440 | tf_op jit(solution)/shard_map/ppermute | solution.py:17
  185.2 11.0 %collective-permute-start.14 = (bf16[2,2,128,1,256]{4,2,1,3,0:T(8,128)(2,1)S(1)}, bf16[2,2,128,1,256]{4,2,1,3,0:T(8,128)(2,1)S(1)}, u32[]{:S(2)}, u32[]{:S(2)}) collective-permute-start(bf16[2,2,128,1,256]{4,2,1,3,0:T(8,128)(2,1)S(1)} %get-tuple-element.269), channel_id=1, source_target_pairs={{0,2},{2,0},{1,3},{3,1},{4,6},{6,4},{5,7},{7,5},{8,10},{10,8},{9,1... | collective-permute-start | bytes 786440 | tf_op jit(solution)/shard_map/ppermute | solution.py:17
  190.2 11.2 %collective-permute-start.5 = (bf16[2,2,128,1,256]{4,2,1,3,0:T(8,128)(2,1)S(1)}, bf16[2,2,128,1,256]{4,2,1,3,0:T(8,128)(2,1)S(1)}, u32[]{:S(2)}, u32[]{:S(2)}) collective-permute-start(bf16[2,2,128,1,256]{4,2,1,3,0:T(8,128)(2,1)S(1)} %get-tuple-element.287), channel_id=1, source_target_pairs={{0,1},{1,0},{2,3},{3,2},{4,5},{5,4},{6,7},{7,6},{8,9},{9,8},{10,11... | collective-permute-start | bytes 786440 | tf_op jit(solution)/shard_map/ppermute | solution.py:17
  196.5 10.5 %collective-permute-start.15 = (bf16[2,2,128,1,256]{4,2,1,3,0:T(8,128)(2,1)S(1)}, bf16[2,2,128,1,256]{4,2,1,3,0:T(8,128)(2,1)S(1)}, u32[]{:S(2)}, u32[]{:S(2)}) collective-permute-start(bf16[2,2,128,1,256]{4,2,1,3,0:T(8,128)(2,1)S(1)} %get-tuple-element.267), channel_id=1, source_target_pairs={{0,1},{1,0},{2,3},{3,2},{4,5},{5,4},{6,7},{7,6},{8,9},{9,8},{10,11... | collective-permute-start | bytes 786440 | tf_op jit(solution)/shard_map/ppermute | solution.py:17
  217.1 7.3 %collective-permute-start.6 = (bf16[2,2,128,1,256]{4,2,1,3,0:T(8,128)(2,1)S(1)}, bf16[2,2,128,1,256]{4,2,1,3,0:T(8,128)(2,1)S(1)}, u32[]{:S(2)}, u32[]{:S(2)}) collective-permute-start(bf16[2,2,128,1,256]{4,2,1,3,0:T(8,128)(2,1)S(1)} %pad_maximum_fusion.5), channel_id=1, source_target_pairs={{0,1},{1,0},{2,3},{3,2},{4,5},{5,4},{6,7},{7,6},{8,9},{9,8},{10,11... | collective-permute-start | bytes 786440 | tf_op jit(solution)/shard_map/ppermute | solution.py:17
  224.7 10.3 %collective-permute-start.7 = (bf16[2,2,128,1,256]{4,2,1,3,0:T(8,128)(2,1)S(1)}, bf16[2,2,128,1,256]{4,2,1,3,0:T(8,128)(2,1)S(1)}, u32[]{:S(2)}, u32[]{:S(2)}) collective-permute-start(bf16[2,2,128,1,256]{4,2,1,3,0:T(8,128)(2,1)S(1)} %get-tuple-element.281), channel_id=1, source_target_pairs={{0,2},{2,0},{1,3},{3,1},{4,6},{6,4},{5,7},{7,5},{8,10},{10,8},{9,1... | collective-permute-start | bytes 786440 | tf_op jit(solution)/shard_map/ppermute | solution.py:17
  235.2 7.1 %collective-permute-start.8 = (bf16[2,2,128,1,256]{4,2,1,3,0:T(8,128)(2,1)S(1)}, bf16[2,2,128,1,256]{4,2,1,3,0:T(8,128)(2,1)S(1)}, u32[]{:S(2)}, u32[]{:S(2)}) collective-permute-start(bf16[2,2,128,1,256]{4,2,1,3,0:T(8,128)(2,1)S(1)} %get-tuple-element.279), channel_id=1, source_target_pairs={{0,4},{4,0},{1,5},{5,1},{2,6},{6,2},{3,7},{7,3},{8,12},{12,8},{9,1... | collective-permute-start | bytes 786440 | tf_op jit(solution)/shard_map/ppermute | solution.py:17
  242.6 10.7 %collective-permute-start.9 = (bf16[2,2,128,1,256]{4,2,1,3,0:T(8,128)(2,1)S(1)}, bf16[2,2,128,1,256]{4,2,1,3,0:T(8,128)(2,1)S(1)}, u32[]{:S(2)}, u32[]{:S(2)}) collective-permute-start(bf16[2,2,128,1,256]{4,2,1,3,0:T(8,128)(2,1)S(1)} %get-tuple-element.277), channel_id=1, source_target_pairs={{0,8},{8,0},{1,9},{9,1},{2,10},{10,2},{3,11},{11,3},{4,12},{12,4},... | collective-permute-start | bytes 786440 | tf_op jit(solution)/shard_map/ppermute | solution.py:17
  253.6 11.8 %collective-permute-start.10 = (bf16[2,2,128,1,256]{4,2,1,3,0:T(8,128)(2,1)S(1)}, bf16[2,2,128,1,256]{4,2,1,3,0:T(8,128)(2,1)S(1)}, u32[]{:S(2)}, u32[]{:S(2)}) collective-permute-start(bf16[2,2,128,1,256]{4,2,1,3,0:T(8,128)(2,1)S(1)} %get-tuple-element.275), channel_id=1, source_target_pairs={{0,16},{16,0},{1,17},{17,1},{2,18},{18,2},{3,19},{19,3},{4,20},{20... | collective-permute-start | bytes 786440 | tf_op jit(solution)/shard_map/ppermute | solution.py:17
  258.5 9.4 %collective-permute-start.16 = (bf16[2,2,128,1,256]{4,2,1,3,0:T(8,128)(2,1)S(1)}, bf16[2,2,128,1,256]{4,2,1,3,0:T(8,128)(2,1)S(1)}, u32[]{:S(2)}, u32[]{:S(2)}) collective-permute-start(bf16[2,2,128,1,256]{4,2,1,3,0:T(8,128)(2,1)S(1)} %pad_maximum_fusion.6), channel_id=1, source_target_pairs={{0,1},{1,0},{2,3},{3,2},{4,5},{5,4},{6,7},{7,6},{8,9},{9,8},{10,11... | collective-permute-start | bytes 786440 | tf_op jit(solution)/shard_map/ppermute | solution.py:17
  268.1 10.2 %collective-permute-start.17 = (bf16[2,2,128,1,256]{4,2,1,3,0:T(8,128)(2,1)S(1)}, bf16[2,2,128,1,256]{4,2,1,3,0:T(8,128)(2,1)S(1)}, u32[]{:S(2)}, u32[]{:S(2)}) collective-permute-start(bf16[2,2,128,1,256]{4,2,1,3,0:T(8,128)(2,1)S(1)} %get-tuple-element.261), channel_id=1, source_target_pairs={{0,2},{2,0},{1,3},{3,1},{4,6},{6,4},{5,7},{7,5},{8,10},{10,8},{9,1... | collective-permute-start | bytes 786440 | tf_op jit(solution)/shard_map/ppermute | solution.py:17
  278.6 7.1 %collective-permute-start.18 = (bf16[2,2,128,1,256]{4,2,1,3,0:T(8,128)(2,1)S(1)}, bf16[2,2,128,1,256]{4,2,1,3,0:T(8,128)(2,1)S(1)}, u32[]{:S(2)}, u32[]{:S(2)}) collective-permute-start(bf16[2,2,128,1,256]{4,2,1,3,0:T(8,128)(2,1)S(1)} %get-tuple-element.259), channel_id=1, source_target_pairs={{0,4},{4,0},{1,5},{5,1},{2,6},{6,2},{3,7},{7,3},{8,12},{12,8},{9,1... | collective-permute-start | bytes 786440 | tf_op jit(solution)/shard_map/ppermute | solution.py:17
  286.0 11.4 %collective-permute-start.19 = (bf16[2,2,128,1,256]{4,2,1,3,0:T(8,128)(2,1)S(1)}, bf16[2,2,128,1,256]{4,2,1,3,0:T(8,128)(2,1)S(1)}, u32[]{:S(2)}, u32[]{:S(2)}) collective-permute-start(bf16[2,2,128,1,256]{4,2,1,3,0:T(8,128)(2,1)S(1)} %get-tuple-element.257), channel_id=1, source_target_pairs={{0,8},{8,0},{1,9},{9,1},{2,10},{10,2},{3,11},{11,3},{4,12},{12,4},... | collective-permute-start | bytes 786440 | tf_op jit(solution)/shard_map/ppermute | solution.py:17
  297.8 13.6 %collective-permute-start.20 = (bf16[2,2,128,1,256]{4,2,1,3,0:T(8,128)(2,1)S(1)}, bf16[2,2,128,1,256]{4,2,1,3,0:T(8,128)(2,1)S(1)}, u32[]{:S(2)}, u32[]{:S(2)}) collective-permute-start(bf16[2,2,128,1,256]{4,2,1,3,0:T(8,128)(2,1)S(1)} %get-tuple-element.255), channel_id=1, source_target_pairs={{0,16},{16,0},{1,17},{17,1},{2,18},{18,2},{3,19},{19,3},{4,20},{20... | collective-permute-start | bytes 786440 | tf_op jit(solution)/shard_map/ppermute | solution.py:17
  311.8 4.8 %collective-permute-start.21 = (f32[2,3,256]{2,0,1:T(2,128)S(1)}, f32[2,3,256]{2,0,1:T(2,128)S(1)}, u32[]{:S(2)}, u32[]{:S(2)}) collective-permute-start(f32[2,3,256]{2,0,1:T(2,128)S(1)} %slice.482), channel_id=1, source_target_pairs={{1,0},{2,1},{3,2},{4,3},{5,4},{6,5},{7,6},{8,7},{9,8},{10,9},{11,1... | collective-permute-start | bytes 18440 | tf_op jit(solution)/shard_map/ppermute | solution.py:23
  (5 other events, 173.7 us)
Sparse Core Ops, SparseCore 0:
  11.0 95.0 all-gather.1
  267.9 79.3 reduce-scatter.1
where the time goes:
time: 357 us; the launch traced here: 354 us
  waiting for transfers between devices  195 us (55%)
  starting transfers between devices  81.9 us (23%)
  other arithmetic  41.7 us (12%)
  matrix products  17 us (5%)
  between operations  15.9 us (4%)
    ppermute x20, waiting for transfers between devices, swapped(): return lax.ppermute(block, axis, route)  82.4 us
    all_gather x1, waiting for transfers between devices, per_device(): w_full = lax.all_gather(w_out, 'ctx', axis=1, tiled=True)  78.2 us
    ppermute x20, starting transfers between devices, swapped(): return lax.ppermute(block, axis, route)  77.5 us
    reduce_scatter x1, waiting for transfers between devices, per_device(): lax.psum_scatter(partial_sum.astype(jnp.bfloat16), 'fsdp', scatter_dimens...  29.9 us
    mul x16, other arithmetic, add_mode(): denom_im = decay_now * full_sine  12.1 us
    mul x16, other arithmetic, add_mode(): lax.dynamic_slice_in_dim(residues, mode_index, 1, 1)[:, 0]  11.8 us
  transfers between devices with their start and end apart: 24, of which 19 were waited for; matrix products, arithmetic and copies ran while one was open for 13% of the time, Pallas kernels for 0%

commit v1 on v0

--- a/solution.py
+++ b/solution.py
@@ -190,7 +190,8 @@
     conv_im = signal_re * filter_im + signal_im * filter_re
     convolved = from_spectrum(conv_re, conv_im)[:, 0]
     gated_out = (query_part * convolved).astype(jnp.bfloat16)
-    w_full = lax.all_gather(w_out, "ctx", axis=1, tiled=True)
+    outgoing = jnp.stack([w_out] * lax.axis_size("ctx"))
+    w_full = jnp.concatenate(lax.all_to_all(outgoing, "ctx", 0, 0), axis=1)
     partial_sum = jnp.dot(gated_out, w_full, preferred_element_type=jnp.float32)
     block_output = lax.psum_scatter(
         partial_sum.astype(jnp.bfloat16), "fsdp", scatter_dimension=1, tiled=True

time: 357 us -> 370 us (1.036)
  the two profiles are of different devices: /device:TPU:25 before, /device:TPU:27 now
where the time goes in v1:
time: 370 us; the launch traced here: 367 us
  waiting for transfers between devices  180 us (49%)
  starting transfers between devices  105 us (28%)
  other arithmetic  41.6 us (11%)
  matrix products  19.2 us (5%)
  between operations  15.9 us (4%)
  local copies, waits for them, and re-layouts  4.57 us (1%)
    ppermute x20, starting transfers between devices, swapped(): return lax.ppermute(block, axis, route)  86.4 us
    all_to_all x1, waiting for transfers between devices, per_device(): w_full = jnp.concatenate(lax.all_to_all(outgoing, 'ctx', 0, 0), axis=1)  73.7 us
    ppermute x20, waiting for transfers between devices, swapped(): return lax.ppermute(block, axis, route)  72.9 us
    reduce_scatter x1, waiting for transfers between devices, per_device(): lax.psum_scatter(partial_sum.astype(jnp.bfloat16), 'fsdp', scatter_dimens...  24 us
    all_to_all x1, starting transfers between devices, per_device(): w_full = jnp.concatenate(lax.all_to_all(outgoing, 'ctx', 0, 0), axis=1)  13.1 us
    mul x16, other arithmetic, add_mode(): denom_im = decay_now * full_sine  12.8 us
    mul x16, other arithmetic, add_mode(): lax.dynamic_slice_in_dim(residues, mode_index, 1, 1)[:, 0]  11.8 us
    ppermute x2, waiting for transfers between devices, shifted(): return lax.ppermute(block, axis, route)  9.54 us
  transfers between devices with their start and end apart: 24, of which 21 were waited for; matrix products, arithmetic and copies ran while one was open for 13% of the time, Pallas kernels for 0%

profile of v1, /device:TPU:27, one launch (start us, length us, event | category | flops | bytes accessed | tf_op | source)
XLA Modules:
  0.0 367.4 jit_solution(3908873842958064139)
XLA Ops:
  10.9 13.1 %all-to-all-start = ((bf16[32,256,256]{1,2,0:T(8,128)(2,1)}), bf16[32,256,256]{1,2,0:T(8,128)(2,1)}, u32[]{:S(2)}, u32[]{:S(2)}) async-start(bf16[32,256,256]{1,2,0:T(8,128)(2,1)} %stack.298), calls=%async_computation | async-start | bytes 8388608 | tf_op jit(solution)/shard_map/all_to_all | solution.py:194
  28.0 5.8 %collective-permute-done = bf16[2,3,256]{2,0,1:T(2,128)(2,1)S(1)} collective-permute-done((bf16[2,3,256]{2,0,1:T(2,128)(2,1)S(1)}, bf16[2,3,256]{2,0,1:T(2,128)(2,1)S(1)}, u32[]{:S(2)}, u32[]{:S(2)}) %collective-permute-start) | collective-permute-done | bytes 3104 | tf_op jit(solution)/shard_map/ppermute | solution.py:23
  34.7 9.9 %collective-permute-start.1 = (bf16[2,2,128,1,256]{4,2,1,3,0:T(8,128)(2,1)}, bf16[2,2,128,1,256]{4,2,1,3,0:T(8,128)(2,1)}, u32[]{:S(2)}, u32[]{:S(2)}) collective-permute-start(bf16[2,2,128,1,256]{4,2,1,3,0:T(8,128)(2,1)} %fusion.53), channel_id=1, source_target_pairs={{0,16},{16,0},{1,17},{17,1},{2,18},{18,2},{3,19},{19,3},{4,20},{20... | collective-permute-start | bytes 786440 | tf_op jit(solution)/shard_map/ppermute | solution.py:17
  44.7 73.7 %all-to-all-done = bf16[32,256,256]{1,2,0:T(8,128)(2,1)} async-done(((bf16[32,256,256]{1,2,0:T(8,128)(2,1)}), bf16[32,256,256]{1,2,0:T(8,128)(2,1)}, u32[]{:S(2)}, u32[]{:S(2)}) %all-to-all-start) | async-done | bytes 4194336 | tf_op jit(solution)/shard_map/all_to_all | solution.py:194
  124.0 30.3 %while.18 = (s32[]{:T(128)}, f32[2,128,256]{2,1,0:T(8,128)S(1)}, f32[2,128,256]{2,1,0:T(8,128)S(1)}, f32[256,16]{0,1:T(8,128)}, f32[256,16]{0,1:T(8,128)}, /*ind...) while((s32[]{:T(128)}, f32[2,128,256]{2,1,0:T(8,128)S(1)}, ...), condition=%wide.region_1.2_spmd.clone.clone.clone, body=%wide.region_0.1_spmd.clone.clone.clone.sunk | while | flops 921377 | bytes 1070735 | solution.py:160
  158.3 10.6 %collective-permute-start.2 = (bf16[2,2,128,1,256]{4,2,1,3,0:T(8,128)(2,1)}, bf16[2,2,128,1,256]{4,2,1,3,0:T(8,128)(2,1)S(1)}, u32[]{:S(2)}, u32[]{:S(2)}) collective-permute-start(bf16[2,2,128,1,256]{4,2,1,3,0:T(8,128)(2,1)} %get-tuple-element.293), channel_id=1, source_target_pairs={{0,8},{8,0},{1,9},{9,1},{2,10},{10,2},{3,11},{11,3},{4,12},{12,4},... | collective-permute-start | bytes 786440 | tf_op jit(solution)/shard_map/ppermute | solution.py:17
  172.8 9.3 %collective-permute-done.2 = bf16[2,2,128,1,256]{4,2,1,3,0:T(8,128)(2,1)S(1)} collective-permute-done((bf16[2,2,128,1,256]{4,2,1,3,0:T(8,128)(2,1)}, bf16[2,2,128,1,256]{4,2,1,3,0:T(8,128)(2,1)S(1)}, u32[]{:S(2)}, u32[]{:S(2)}) %collective-permute-start.2) | collective-permute-done | bytes 262176 | tf_op jit(solution)/shard_map/ppermute | solution.py:17
  202.6 4.6 %collective-permute-start.5 = (bf16[2,2,128,1,256]{4,2,1,3,0:T(8,128)(2,1)S(1)}, bf16[2,2,128,1,256]{4,2,1,3,0:T(8,128)(2,1)S(1)}, u32[]{:S(2)}, u32[]{:S(2)}) collective-permute-start(bf16[2,2,128,1,256]{4,2,1,3,0:T(8,128)(2,1)S(1)} %get-tuple-element.287), channel_id=1, source_target_pairs={{0,1},{1,0},{2,3},{3,2},{4,5},{5,4},{6,7},{7,6},{8,9},{9,8},{10,11... | collective-permute-start | bytes 786440 | tf_op jit(solution)/shard_map/ppermute | solution.py:17
  209.0 4.5 %collective-permute-start.15 = (bf16[2,2,128,1,256]{4,2,1,3,0:T(8,128)(2,1)S(1)}, bf16[2,2,128,1,256]{4,2,1,3,0:T(8,128)(2,1)S(1)}, u32[]{:S(2)}, u32[]{:S(2)}) collective-permute-start(bf16[2,2,128,1,256]{4,2,1,3,0:T(8,128)(2,1)S(1)} %get-tuple-element.267), channel_id=1, source_target_pairs={{0,1},{1,0},{2,3},{3,2},{4,5},{5,4},{6,7},{7,6},{8,9},{9,8},{10,11... | collective-permute-start | bytes 786440 | tf_op jit(solution)/shard_map/ppermute | solution.py:17
  231.4 5.2 %collective-permute-done.6 = bf16[2,2,128,1,256]{4,2,1,3,0:T(8,128)(2,1)S(1)} collective-permute-done((bf16[2,2,128,1,256]{4,2,1,3,0:T(8,128)(2,1)S(1)}, bf16[2,2,128,1,256]{4,2,1,3,0:T(8,128)(2,1)S(1)}, u32[]{:S(2)}, u32[]{:S(2)}) %collective-permute-start.6) | collective-permute-done | bytes 262176 | tf_op jit(solution)/shard_map/ppermute | solution.py:17
  236.9 4.3 %collective-permute-start.7 = (bf16[2,2,128,1,256]{4,2,1,3,0:T(8,128)(2,1)S(1)}, bf16[2,2,128,1,256]{4,2,1,3,0:T(8,128)(2,1)S(1)}, u32[]{:S(2)}, u32[]{:S(2)}) collective-permute-start(bf16[2,2,128,1,256]{4,2,1,3,0:T(8,128)(2,1)S(1)} %get-tuple-element.281), channel_id=1, source_target_pairs={{0,2},{2,0},{1,3},{3,1},{4,6},{6,4},{5,7},{7,5},{8,10},{10,8},{9,1... | collective-permute-start | bytes 786440 | tf_op jit(solution)/shard_map/ppermute | solution.py:17
  241.2 4.9 %collective-permute-done.7 = bf16[2,2,128,1,256]{4,2,1,3,0:T(8,128)(2,1)S(1)} collective-permute-done((bf16[2,2,128,1,256]{4,2,1,3,0:T(8,128)(2,1)S(1)}, bf16[2,2,128,1,256]{4,2,1,3,0:T(8,128)(2,1)S(1)}, u32[]{:S(2)}, u32[]{:S(2)}) %collective-permute-start.7) | collective-permute-done | bytes 262176 | tf_op jit(solution)/shard_map/ppermute | solution.py:17
  249.7 4.1 %collective-permute-done.8 = bf16[2,2,128,1,256]{4,2,1,3,0:T(8,128)(2,1)S(1)} collective-permute-done((bf16[2,2,128,1,256]{4,2,1,3,0:T(8,128)(2,1)S(1)}, bf16[2,2,128,1,256]{4,2,1,3,0:T(8,128)(2,1)S(1)}, u32[]{:S(2)}, u32[]{:S(2)}) %collective-permute-start.8) | collective-permute-done | bytes 262176 | tf_op jit(solution)/shard_map/ppermute | solution.py:17
  254.1 4.9 %collective-permute-start.9 = (bf16[2,2,128,1,256]{4,2,1,3,0:T(8,128)(2,1)S(1)}, bf16[2,2,128,1,256]{4,2,1,3,0:T(8,128)(2,1)S(1)}, u32[]{:S(2)}, u32[]{:S(2)}) collective-permute-start(bf16[2,2,128,1,256]{4,2,1,3,0:T(8,128)(2,1)S(1)} %get-tuple-element.277), channel_id=1, source_target_pairs={{0,8},{8,0},{1,9},{9,1},{2,10},{10,2},{3,11},{11,3},{4,12},{12,4},... | collective-permute-start | bytes 786440 | tf_op jit(solution)/shard_map/ppermute | solution.py:17
  259.0 6.6 %collective-permute-done.9 = bf16[2,2,128,1,256]{4,2,1,3,0:T(8,128)(2,1)S(1)} collective-permute-done((bf16[2,2,128,1,256]{4,2,1,3,0:T(8,128)(2,1)S(1)}, bf16[2,2,128,1,256]{4,2,1,3,0:T(8,128)(2,1)S(1)}, u32[]{:S(2)}, u32[]{:S(2)}) %collective-permute-start.9) | collective-permute-done | bytes 262176 | tf_op jit(solution)/shard_map/ppermute | solution.py:17
  265.9 6.2 %collective-permute-start.10 = (bf16[2,2,128,1,256]{4,2,1,3,0:T(8,128)(2,1)S(1)}, bf16[2,2,128,1,256]{4,2,1,3,0:T(8,128)(2,1)S(1)}, u32[]{:S(2)}, u32[]{:S(2)}) collective-permute-start(bf16[2,2,128,1,256]{4,2,1,3,0:T(8,128)(2,1)S(1)} %get-tuple-element.275), channel_id=1, source_target_pairs={{0,16},{16,0},{1,17},{17,1},{2,18},{18,2},{3,19},{19,3},{4,20},{20... | collective-permute-start | bytes 786440 | tf_op jit(solution)/shard_map/ppermute | solution.py:17
  278.0 5.0 %convolution_convert_fusion = bf16[128,8192]{1,0:T(8,128)(2,1)} fusion(bf16[256,8192]{0,1:T(8,128)(2,1)} %bitcast.38, f32[1,1,128,1,256]{4,2,1,3,0:T(8,128)S(1)} %get-tuple-element.252, f32[128,3,256]{2,0,1:T(8,128)S(1)} %fusion.47), kind=kOutput, calls=%fused_computation.28 | convolution fusion | flops 537985024 | bytes 6553600 | tf_op jit(solution)/shard_map/dot_general | solution.py:195
  283.3 5.0 %collective-permute-start.17 = (bf16[2,2,128,1,256]{4,2,1,3,0:T(8,128)(2,1)S(1)}, bf16[2,2,128,1,256]{4,2,1,3,0:T(8,128)(2,1)S(1)}, u32[]{:S(2)}, u32[]{:S(2)}) collective-permute-start(bf16[2,2,128,1,256]{4,2,1,3,0:T(8,128)(2,1)S(1)} %get-tuple-element.261), channel_id=1, source_target_pairs={{0,2},{2,0},{1,3},{3,1},{4,6},{6,4},{5,7},{7,5},{8,10},{10,8},{9,1... | collective-permute-start | bytes 786440 | tf_op jit(solution)/shard_map/ppermute | solution.py:17
  288.3 5.8 %collective-permute-done.17 = bf16[2,2,128,1,256]{4,2,1,3,0:T(8,128)(2,1)S(1)} collective-permute-done((bf16[2,2,128,1,256]{4,2,1,3,0:T(8,128)(2,1)S(1)}, bf16[2,2,128,1,256]{4,2,1,3,0:T(8,128)(2,1)S(1)}, u32[]{:S(2)}, u32[]{:S(2)}) %collective-permute-start.17) | collective-permute-done | bytes 262176 | tf_op jit(solution)/shard_map/ppermute | solution.py:17
  302.5 4.6 %collective-permute-start.19 = (bf16[2,2,128,1,256]{4,2,1,3,0:T(8,128)(2,1)S(1)}, bf16[2,2,128,1,256]{4,2,1,3,0:T(8,128)(2,1)S(1)}, u32[]{:S(2)}, u32[]{:S(2)}) collective-permute-start(bf16[2,2,128,1,256]{4,2,1,3,0:T(8,128)(2,1)S(1)} %get-tuple-element.257), channel_id=1, source_target_pairs={{0,8},{8,0},{1,9},{9,1},{2,10},{10,2},{3,11},{11,3},{4,12},{12,4},... | collective-permute-start | bytes 786440 | tf_op jit(solution)/shard_map/ppermute | solution.py:17
  307.1 6.6 %collective-permute-done.19 = bf16[2,2,128,1,256]{4,2,1,3,0:T(8,128)(2,1)S(1)} collective-permute-done((bf16[2,2,128,1,256]{4,2,1,3,0:T(8,128)(2,1)S(1)}, bf16[2,2,128,1,256]{4,2,1,3,0:T(8,128)(2,1)S(1)}, u32[]{:S(2)}, u32[]{:S(2)}) %collective-permute-start.19) | collective-permute-done | bytes 262176 | tf_op jit(solution)/shard_map/ppermute | solution.py:17
  313.9 6.9 %collective-permute-start.20 = (bf16[2,2,128,1,256]{4,2,1,3,0:T(8,128)(2,1)S(1)}, bf16[2,2,128,1,256]{4,2,1,3,0:T(8,128)(2,1)S(1)}, u32[]{:S(2)}, u32[]{:S(2)}) collective-permute-start(bf16[2,2,128,1,256]{4,2,1,3,0:T(8,128)(2,1)S(1)} %get-tuple-element.255), channel_id=1, source_target_pairs={{0,16},{16,0},{1,17},{17,1},{2,18},{18,2},{3,19},{19,3},{4,20},{20... | collective-permute-start | bytes 786440 | tf_op jit(solution)/shard_map/ppermute | solution.py:17
  320.9 8.0 %collective-permute-done.20 = bf16[2,2,128,1,256]{4,2,1,3,0:T(8,128)(2,1)S(1)} collective-permute-done((bf16[2,2,128,1,256]{4,2,1,3,0:T(8,128)(2,1)S(1)}, bf16[2,2,128,1,256]{4,2,1,3,0:T(8,128)(2,1)S(1)}, u32[]{:S(2)}, u32[]{:S(2)}) %collective-permute-start.20) | collective-permute-done | bytes 262176 | tf_op jit(solution)/shard_map/ppermute | solution.py:17
  336.6 24.0 %reduce-scatter.2.cloned.1.call-done = bf16[128,512]{1,0:T(8,128)(2,1)} async-done(((bf16[128,8192]{1,0:T(8,128)(2,1)}), bf16[128,512]{1,0:T(8,128)(2,1)}) %reduce-scatter.2.cloned.1.call-update) | async-done | bytes 131088 | tf_op jit(solution)/shard_map/reduce_scatter | solution.py:196
  (242 shorter events, 117.5 us)
Async XLA Ops:
  10.9 107.6 %all-to-all-start = ((bf16[32,256,256]{1,2,0:T(8,128)(2,1)}), bf16[32,256,256]{1,2,0:T(8,128)(2,1)}, u32[]{:S(2)}, u32[]{:S(2)}) async-start(bf16[32,256,256]{1,2,0:T(8,128)(2,1)} %stack.298), calls=%async_computation | async-start | bytes 8388608 | tf_op jit(solution)/shard_map/all_to_all | solution.py:194
  23.9 336.6 %reduce-scatter.2.cloned.1.call-start = ((), (), s32[]{:S(2)}) async-start(), calls=%async_computation.2 | async-start | bytes 2228224 | tf_op jit(solution)/shard_map/reduce_scatter | solution.py:196
  24.0 9.7 %collective-permute-start = (bf16[2,3,256]{2,0,1:T(2,128)(2,1)S(1)}, bf16[2,3,256]{2,0,1:T(2,128)(2,1)S(1)}, u32[]{:S(2)}, u32[]{:S(2)}) collective-permute-start(bf16[2,3,256]{2,0,1:T(2,128)(2,1)S(1)} %slice.158), channel_id=1, source_target_pairs={{0,1},{1,2},{2,3},{3,4},{4,5},{5,6},{6,7},{7,8},{8,9},{9,10},{10,1... | collective-permute-start | bytes 9224 | tf_op jit(solution)/shard_map/ppermute | solution.py:23
  34.7 119.7 %collective-permute-start.1 = (bf16[2,2,128,1,256]{4,2,1,3,0:T(8,128)(2,1)}, bf16[2,2,128,1,256]{4,2,1,3,0:T(8,128)(2,1)}, u32[]{:S(2)}, u32[]{:S(2)}) collective-permute-start(bf16[2,2,128,1,256]{4,2,1,3,0:T(8,128)(2,1)} %fusion.53), channel_id=1, source_target_pairs={{0,16},{16,0},{1,17},{17,1},{2,18},{18,2},{3,19},{19,3},{4,20},{20... | collective-permute-start | bytes 786440 | tf_op jit(solution)/shard_map/ppermute | solution.py:17
  122.0 33.4 %collective-permute-start.11 = (bf16[2,2,128,1,256]{4,2,1,3,0:T(8,128)(2,1)S(1)}, bf16[2,2,128,1,256]{4,2,1,3,0:T(8,128)(2,1)S(1)}, u32[]{:S(2)}, u32[]{:S(2)}) collective-permute-start(bf16[2,2,128,1,256]{4,2,1,3,0:T(8,128)(2,1)S(1)} %fusion.52), channel_id=1, source_target_pairs={{0,16},{16,0},{1,17},{17,1},{2,18},{18,2},{3,19},{19,3},{4,20},{20... | collective-permute-start | bytes 786440 | tf_op jit(solution)/shard_map/ppermute | solution.py:17
  158.3 23.8 %collective-permute-start.2 = (bf16[2,2,128,1,256]{4,2,1,3,0:T(8,128)(2,1)}, bf16[2,2,128,1,256]{4,2,1,3,0:T(8,128)(2,1)S(1)}, u32[]{:S(2)}, u32[]{:S(2)}) collective-permute-start(bf16[2,2,128,1,256]{4,2,1,3,0:T(8,128)(2,1)} %get-tuple-element.293), channel_id=1, source_target_pairs={{0,8},{8,0},{1,9},{9,1},{2,10},{10,2},{3,11},{11,3},{4,12},{12,4},... | collective-permute-start | bytes 786440 | tf_op jit(solution)/shard_map/ppermute | solution.py:17
  170.9 16.8 %collective-permute-start.12 = (bf16[2,2,128,1,256]{4,2,1,3,0:T(8,128)(2,1)S(1)}, bf16[2,2,128,1,256]{4,2,1,3,0:T(8,128)(2,1)S(1)}, u32[]{:S(2)}, u32[]{:S(2)}) collective-permute-start(bf16[2,2,128,1,256]{4,2,1,3,0:T(8,128)(2,1)S(1)} %get-tuple-element.273), channel_id=1, source_target_pairs={{0,8},{8,0},{1,9},{9,1},{2,10},{10,2},{3,11},{11,3},{4,12},{12,4},... | collective-permute-start | bytes 786440 | tf_op jit(solution)/shard_map/ppermute | solution.py:17
  182.3 10.5 %collective-permute-start.3 = (bf16[2,2,128,1,256]{4,2,1,3,0:T(8,128)(2,1)S(1)}, bf16[2,2,128,1,256]{4,2,1,3,0:T(8,128)(2,1)S(1)}, u32[]{:S(2)}, u32[]{:S(2)}) collective-permute-start(bf16[2,2,128,1,256]{4,2,1,3,0:T(8,128)(2,1)S(1)} %get-tuple-element.291), channel_id=1, source_target_pairs={{0,4},{4,0},{1,5},{5,1},{2,6},{6,2},{3,7},{7,3},{8,12},{12,8},{9,1... | collective-permute-start | bytes 786440 | tf_op jit(solution)/shard_map/ppermute | solution.py:17
  188.0 10.5 %collective-permute-start.13 = (bf16[2,2,128,1,256]{4,2,1,3,0:T(8,128)(2,1)S(1)}, bf16[2,2,128,1,256]{4,2,1,3,0:T(8,128)(2,1)S(1)}, u32[]{:S(2)}, u32[]{:S(2)}) collective-permute-start(bf16[2,2,128,1,256]{4,2,1,3,0:T(8,128)(2,1)S(1)} %get-tuple-element.271), channel_id=1, source_target_pairs={{0,4},{4,0},{1,5},{5,1},{2,6},{6,2},{3,7},{7,3},{8,12},{12,8},{9,1... | collective-permute-start | bytes 786440 | tf_op jit(solution)/shard_map/ppermute | solution.py:17
  193.0 9.3 %collective-permute-start.4 = (bf16[2,2,128,1,256]{4,2,1,3,0:T(8,128)(2,1)S(1)}, bf16[2,2,128,1,256]{4,2,1,3,0:T(8,128)(2,1)S(1)}, u32[]{:S(2)}, u32[]{:S(2)}) collective-permute-start(bf16[2,2,128,1,256]{4,2,1,3,0:T(8,128)(2,1)S(1)} %get-tuple-element.289), channel_id=1, source_target_pairs={{0,2},{2,0},{1,3},{3,1},{4,6},{6,4},{5,7},{7,5},{8,10},{10,8},{9,1... | collective-permute-start | bytes 786440 | tf_op jit(solution)/shard_map/ppermute | solution.py:17
  198.7 10.1 %collective-permute-start.14 = (bf16[2,2,128,1,256]{4,2,1,3,0:T(8,128)(2,1)S(1)}, bf16[2,2,128,1,256]{4,2,1,3,0:T(8,128)(2,1)S(1)}, u32[]{:S(2)}, u32[]{:S(2)}) collective-permute-start(bf16[2,2,128,1,256]{4,2,1,3,0:T(8,128)(2,1)S(1)} %get-tuple-element.269), channel_id=1, source_target_pairs={{0,2},{2,0},{1,3},{3,1},{4,6},{6,4},{5,7},{7,5},{8,10},{10,8},{9,1... | collective-permute-start | bytes 786440 | tf_op jit(solution)/shard_map/ppermute | solution.py:17
  202.6 12.4 %collective-permute-start.5 = (bf16[2,2,128,1,256]{4,2,1,3,0:T(8,128)(2,1)S(1)}, bf16[2,2,128,1,256]{4,2,1,3,0:T(8,128)(2,1)S(1)}, u32[]{:S(2)}, u32[]{:S(2)}) collective-permute-start(bf16[2,2,128,1,256]{4,2,1,3,0:T(8,128)(2,1)S(1)} %get-tuple-element.287), channel_id=1, source_target_pairs={{0,1},{1,0},{2,3},{3,2},{4,5},{5,4},{6,7},{7,6},{8,9},{9,8},{10,11... | collective-permute-start | bytes 786440 | tf_op jit(solution)/shard_map/ppermute | solution.py:17
  209.0 10.4 %collective-permute-start.15 = (bf16[2,2,128,1,256]{4,2,1,3,0:T(8,128)(2,1)S(1)}, bf16[2,2,128,1,256]{4,2,1,3,0:T(8,128)(2,1)S(1)}, u32[]{:S(2)}, u32[]{:S(2)}) collective-permute-start(bf16[2,2,128,1,256]{4,2,1,3,0:T(8,128)(2,1)S(1)} %get-tuple-element.267), channel_id=1, source_target_pairs={{0,1},{1,0},{2,3},{3,2},{4,5},{5,4},{6,7},{7,6},{8,9},{9,8},{10,11... | collective-permute-start | bytes 786440 | tf_op jit(solution)/shard_map/ppermute | solution.py:17
  229.5 7.1 %collective-permute-start.6 = (bf16[2,2,128,1,256]{4,2,1,3,0:T(8,128)(2,1)S(1)}, bf16[2,2,128,1,256]{4,2,1,3,0:T(8,128)(2,1)S(1)}, u32[]{:S(2)}, u32[]{:S(2)}) collective-permute-start(bf16[2,2,128,1,256]{4,2,1,3,0:T(8,128)(2,1)S(1)} %pad_maximum_fusion.5), channel_id=1, source_target_pairs={{0,1},{1,0},{2,3},{3,2},{4,5},{5,4},{6,7},{7,6},{8,9},{9,8},{10,11... | collective-permute-start | bytes 786440 | tf_op jit(solution)/shard_map/ppermute | solution.py:17
  236.9 9.2 %collective-permute-start.7 = (bf16[2,2,128,1,256]{4,2,1,3,0:T(8,128)(2,1)S(1)}, bf16[2,2,128,1,256]{4,2,1,3,0:T(8,128)(2,1)S(1)}, u32[]{:S(2)}, u32[]{:S(2)}) collective-permute-start(bf16[2,2,128,1,256]{4,2,1,3,0:T(8,128)(2,1)S(1)} %get-tuple-element.281), channel_id=1, source_target_pairs={{0,2},{2,0},{1,3},{3,1},{4,6},{6,4},{5,7},{7,5},{8,10},{10,8},{9,1... | collective-permute-start | bytes 786440 | tf_op jit(solution)/shard_map/ppermute | solution.py:17
  246.4 7.4 %collective-permute-start.8 = (bf16[2,2,128,1,256]{4,2,1,3,0:T(8,128)(2,1)S(1)}, bf16[2,2,128,1,256]{4,2,1,3,0:T(8,128)(2,1)S(1)}, u32[]{:S(2)}, u32[]{:S(2)}) collective-permute-start(bf16[2,2,128,1,256]{4,2,1,3,0:T(8,128)(2,1)S(1)} %get-tuple-element.279), channel_id=1, source_target_pairs={{0,4},{4,0},{1,5},{5,1},{2,6},{6,2},{3,7},{7,3},{8,12},{12,8},{9,1... | collective-permute-start | bytes 786440 | tf_op jit(solution)/shard_map/ppermute | solution.py:17
  254.1 11.5 %collective-permute-start.9 = (bf16[2,2,128,1,256]{4,2,1,3,0:T(8,128)(2,1)S(1)}, bf16[2,2,128,1,256]{4,2,1,3,0:T(8,128)(2,1)S(1)}, u32[]{:S(2)}, u32[]{:S(2)}) collective-permute-start(bf16[2,2,128,1,256]{4,2,1,3,0:T(8,128)(2,1)S(1)} %get-tuple-element.277), channel_id=1, source_target_pairs={{0,8},{8,0},{1,9},{9,1},{2,10},{10,2},{3,11},{11,3},{4,12},{12,4},... | collective-permute-start | bytes 786440 | tf_op jit(solution)/shard_map/ppermute | solution.py:17
  265.9 11.8 %collective-permute-start.10 = (bf16[2,2,128,1,256]{4,2,1,3,0:T(8,128)(2,1)S(1)}, bf16[2,2,128,1,256]{4,2,1,3,0:T(8,128)(2,1)S(1)}, u32[]{:S(2)}, u32[]{:S(2)}) collective-permute-start(bf16[2,2,128,1,256]{4,2,1,3,0:T(8,128)(2,1)S(1)} %get-tuple-element.275), channel_id=1, source_target_pairs={{0,16},{16,0},{1,17},{17,1},{2,18},{18,2},{3,19},{19,3},{4,20},{20... | collective-permute-start | bytes 786440 | tf_op jit(solution)/shard_map/ppermute | solution.py:17
  272.1 11.0 %collective-permute-start.16 = (bf16[2,2,128,1,256]{4,2,1,3,0:T(8,128)(2,1)S(1)}, bf16[2,2,128,1,256]{4,2,1,3,0:T(8,128)(2,1)S(1)}, u32[]{:S(2)}, u32[]{:S(2)}) collective-permute-start(bf16[2,2,128,1,256]{4,2,1,3,0:T(8,128)(2,1)S(1)} %pad_maximum_fusion.6), channel_id=1, source_target_pairs={{0,1},{1,0},{2,3},{3,2},{4,5},{5,4},{6,7},{7,6},{8,9},{9,8},{10,11... | collective-permute-start | bytes 786440 | tf_op jit(solution)/shard_map/ppermute | solution.py:17
  283.3 10.8 %collective-permute-start.17 = (bf16[2,2,128,1,256]{4,2,1,3,0:T(8,128)(2,1)S(1)}, bf16[2,2,128,1,256]{4,2,1,3,0:T(8,128)(2,1)S(1)}, u32[]{:S(2)}, u32[]{:S(2)}) collective-permute-start(bf16[2,2,128,1,256]{4,2,1,3,0:T(8,128)(2,1)S(1)} %get-tuple-element.261), channel_id=1, source_target_pairs={{0,2},{2,0},{1,3},{3,1},{4,6},{6,4},{5,7},{7,5},{8,10},{10,8},{9,1... | collective-permute-start | bytes 786440 | tf_op jit(solution)/shard_map/ppermute | solution.py:17
  294.4 7.8 %collective-permute-start.18 = (bf16[2,2,128,1,256]{4,2,1,3,0:T(8,128)(2,1)S(1)}, bf16[2,2,128,1,256]{4,2,1,3,0:T(8,128)(2,1)S(1)}, u32[]{:S(2)}, u32[]{:S(2)}) collective-permute-start(bf16[2,2,128,1,256]{4,2,1,3,0:T(8,128)(2,1)S(1)} %get-tuple-element.259), channel_id=1, source_target_pairs={{0,4},{4,0},{1,5},{5,1},{2,6},{6,2},{3,7},{7,3},{8,12},{12,8},{9,1... | collective-permute-start | bytes 786440 | tf_op jit(solution)/shard_map/ppermute | solution.py:17
  302.5 11.2 %collective-permute-start.19 = (bf16[2,2,128,1,256]{4,2,1,3,0:T(8,128)(2,1)S(1)}, bf16[2,2,128,1,256]{4,2,1,3,0:T(8,128)(2,1)S(1)}, u32[]{:S(2)}, u32[]{:S(2)}) collective-permute-start(bf16[2,2,128,1,256]{4,2,1,3,0:T(8,128)(2,1)S(1)} %get-tuple-element.257), channel_id=1, source_target_pairs={{0,8},{8,0},{1,9},{9,1},{2,10},{10,2},{3,11},{11,3},{4,12},{12,4},... | collective-permute-start | bytes 786440 | tf_op jit(solution)/shard_map/ppermute | solution.py:17
  313.9 14.9 %collective-permute-start.20 = (bf16[2,2,128,1,256]{4,2,1,3,0:T(8,128)(2,1)S(1)}, bf16[2,2,128,1,256]{4,2,1,3,0:T(8,128)(2,1)S(1)}, u32[]{:S(2)}, u32[]{:S(2)}) collective-permute-start(bf16[2,2,128,1,256]{4,2,1,3,0:T(8,128)(2,1)S(1)} %get-tuple-element.255), channel_id=1, source_target_pairs={{0,16},{16,0},{1,17},{17,1},{2,18},{18,2},{3,19},{19,3},{4,20},{20... | collective-permute-start | bytes 786440 | tf_op jit(solution)/shard_map/ppermute | solution.py:17
  329.2 6.6 %collective-permute-start.21 = (f32[2,3,256]{2,0,1:T(2,128)S(1)}, f32[2,3,256]{2,0,1:T(2,128)S(1)}, u32[]{:S(2)}, u32[]{:S(2)}) collective-permute-start(f32[2,3,256]{2,0,1:T(2,128)S(1)} %slice.482), channel_id=1, source_target_pairs={{1,0},{2,1},{3,2},{4,3},{5,4},{6,5},{7,6},{8,7},{9,8},{10,9},{11,1... | collective-permute-start | bytes 18440 | tf_op jit(solution)/shard_map/ppermute | solution.py:23
  (6 other events, 201.0 us)
Sparse Core Ops, SparseCore 0:
  283.1 77.4 reduce-scatter.1
